TPU v7x, 32 devices: a whole 2x2x4 slice. The times are simulated.
32 devices in a mesh: ka: 2 (over core), pair: 16 (over z, y, x).
Axes of the slice: x: 2, y: 2, z: 4, core: 2. Of those that a mesh axis runs over, the one named last changes fastest.
Arguments:
- cond_orbitals: bfloat16 [2, 2048, 2048], P('ka', 'pair'), may hold values from -6 to 6
- cond_energy: float32 [2, 2048], P('ka', 'pair'), may hold values from 0.5 to 8
- val_orbitals: bfloat16 [32, 2048], P(('ka', 'pair')), may hold values from -6 to 6
- val_energy: bfloat16 [32], P(('ka', 'pair')), may hold values from -8 to -0.5
- val_slots: int32 [2, 16, 16], P('ka', 'pair'), may hold values from 0 to 31
- owner_count: int32 [2, 16], P('ka', 'pair'), may hold values from 1 to 16, as said below
Outputs:
- response: float32 [2, 2048, 512], P('ka', 'pair')
Inputs may be any that keep to these rules, and one draw needn't show every extreme that they name: `owner_count`: in every lane some owner has exactly 16 live slots.
All inputs are finite; a program needn't handle non-finite values.
Results may differ from a plain program's by a relative error of at most 0.0047.
The roundings to bfloat16 on the way count: a program that leaves them out, or rounds other values in their place, can miss the bound.
Values may be sent and summed in bfloat16 or wider, within the bound.
A program may use at most 64 MiB of HBM per device.

v0:
```python
import jax
import jax.numpy as jnp
from jax import lax
from jax.sharding import PartitionSpec as P

BC = 128
GA = 16
GB = 128
WIN = 512
SLOTS = 16


def cosine_table(length):
    freq = lax.iota(jnp.float32, length)[:, None]
    point = lax.iota(jnp.float32, length)[None, :]
    factor = jnp.where(freq == 0, jnp.sqrt(1.0 / length), jnp.sqrt(2.0 / length))
    return (factor * jnp.cos(jnp.pi * (point + 0.5) * freq / length)).astype(jnp.bfloat16)


def owner_terms(picked, e_pick, live, cond_block, e_cond, table_a, table_b):
    slots = picked.shape[0]
    pair_real = (
        picked[:, None, :].astype(jnp.float32) * cond_block[None].astype(jnp.float32)
    ).astype(jnp.bfloat16)
    count = slots * cond_block.shape[0]
    rows = pair_real.reshape(count * GA, GB)
    first = jnp.dot(rows, table_b.T, preferred_element_type=jnp.float32).astype(jnp.bfloat16)
    first = first.reshape(count, GA, GB)
    moved = jnp.einsum("ja,pak->pjk", table_a, first, preferred_element_type=jnp.float32)
    moved = moved.astype(jnp.bfloat16).reshape(count, GA * GB)
    weight = live[:, None] * 2.0 / (e_cond[None, :] - e_pick[:, None])
    weighted = (moved[:, :WIN].astype(jnp.float32) * weight.reshape(count, 1)).astype(jnp.bfloat16)
    return (moved, weighted)


def shards(cond_orbitals, cond_energy, val_orbitals, val_energy, val_slots, owner_count):
    cond_block = lax.all_to_all(cond_orbitals, "pair", split_axis=2, concat_axis=1, tiled=True)[0].T
    all_orb, all_energy = (
        lax.all_gather(val_orbitals, ("ka", "pair"), axis=0, tiled=True),
        lax.all_gather(val_energy, ("ka", "pair"), axis=0, tiled=True),
    )
    slots = val_slots[0, 0]
    picked = jnp.take(all_orb, slots, axis=0)
    e_pick = jnp.take(all_energy, slots).astype(jnp.float32)
    live = (lax.iota(jnp.int32, slots.shape[0]) < owner_count[0, 0]).astype(jnp.float32)
    moved, weighted = owner_terms(
        picked, e_pick, live, cond_block, cond_energy[0], cosine_table(GA), cosine_table(GB)
    )
    owners = lax.axis_size("pair")
    mine = lax.psum_scatter(
        lax.dot_general(
            moved, weighted, (((0,), (0,)), ((), ())), preferred_element_type=jnp.float32
        ),
        "pair",
        scatter_dimension=0,
        tiled=True,
    )
    scale = 2.0 / (SLOTS * BC * owners)
    return (mine * scale)[None]


def solution(mesh):
    return jax.shard_map(
        shards,
        mesh=mesh,
        in_specs=(
            P("ka", "pair", None),
            P("ka", "pair"),
            P(("ka", "pair"), None),
            P(("ka", "pair")),
            P("ka", "pair", None),
            P("ka", "pair"),
        ),
        out_specs=P("ka", "pair", None),
        check_vma=False,
    )
```

profile of v0, /device:TPU:0, one launch (start us, length us, event | category | flops | bytes accessed | tf_op | source)
XLA Modules:
  0.0 298.1 jit_solution(10170052519686423794)
XLA Ops:
  6.5 2.3 copy.15
  8.9 0.5 broadcast.173
  9.4 11.5 %reduce = bf16[2048,128]{1,0:T(8,128)(2,1)S(1)} reduce(bf16[2048,1,128]{2,1,0:T(2,128)(2,1)S(1)} %bitcast.43, bf16[]{:T(256)} %broadcast.173), dimensions={1}, to_apply=%bitcast.30.reduce_sub_computation | reduce | bytes 1048578
  20.9 0.9 reshape.162
  21.8 8.3 %all-to-all-start = ((bf16[16,2,8192]{2,1,0:T(2,128)(2,1)}), bf16[16,2,8192]{2,1,0:T(2,128)(2,1)S(1)}, u32[]{:S(2)}, u32[]{:S(2)}) async-start(bf16[16,2,8192]{2,1,0:T(2,128)(2,1)} %reshape.162), calls=%async_computation | async-start | bytes 1048576 | tf_op jit(solution)/shard_map/all_to_all | solution.py:37
  30.2 0.0 reduce-scatter.2.cloned.1.call-start
  30.3 0.7 fusion.11
  31.6 0.1 dynamic-update-slice
  31.7 41.0 %all-reduce = bf16[32]{0:T(256)(128)(2,1)S(1)} all-reduce(bf16[32]{0:T(256)(128)(2,1)S(1)} %dynamic-update-slice), channel_id=1, replica_groups=mesh['ka'=2,'pair'=16] {'ka','pair'}, use_global_device_ids=true, to_apply=%add | all-reduce | flops 32 | bytes 128
  72.7 67.5 %all-gather = bf16[32,1,2048]{2,1,0:T(2,128)(2,1)S(1)} all-gather(bf16[1,1,2048]{2,1,0:T(2,128)(2,1)} %bitcast.47), channel_id=1, replica_groups=mesh['ka'=2,'pair'=16] {'ka','pair'}, dimensions={0}, use_global_device_ids=true | all-gather | bytes 135168 | tf_op jit(solution)/shard_map/all_gather | solution.py:39
  140.2 0.1 copy.24
  140.3 0.7 gather_fusion.1
  141.0 0.6 gather_fusion
  142.2 0.7 select_convert_fusion.1
  142.9 0.7 divide_bitcast_fusion
  143.6 0.1 select_convert_fusion
  143.7 0.0 all-to-all-done
  143.7 0.5 reshape.163
  144.3 0.1 copy.16
  144.3 0.1 convert_bitcast_fusion
  144.4 0.3 copy.17
  144.8 0.3 copy.18
  145.1 5.4 %multiply_convert_fusion = bf16[16,128,2048]{2,1,0:T(8,128)(2,1)} fusion(f32[128,2048]{1,0:T(8,128)S(1)} %copy.18, f32[16,2048]{1,0:T(8,128)S(1)} %select_convert_fusion), kind=kLoop, calls=%fused_computation.3 | loop fusion | flops 8388608 | bytes 9568256 | tf_op jit(solution)/shard_map/convert_element_type | solution.py:24
  150.5 13.5 %convert_element_type.68 = bf16[32768,128]{1,0:T(8,128)(2,1)} reshape(bf16[16,128,2048]{2,1,0:T(8,128)(2,1)} %multiply_convert_fusion) | data formatting | bytes 16777216 | tf_op jit(solution)/shard_map/convert_element_type | solution.py:24
  164.0 5.9 %convolution_convert_fusion = bf16[32768,128]{1,0:T(8,128)(2,1)S(1)} fusion(bf16[32768,128]{1,0:T(8,128)(2,1)} %convert_element_type.68, f32[128]{0:T(128)S(1)} %get-tuple-element.8, f32[128]{0:T(128)S(1)} %get-tuple-element.7), kind=kOutput, calls=%fused_computation.2 | convolution fusion | flops 1078001664 | bytes 16778240 | tf_op jit(solution)/shard_map/dot_general | solution.py:27
  169.9 5.6 %convolution_convert_fusion.1 = bf16[2048,128,16]{1,2,0:T(8,128)(2,1)} fusion(bf16[2048,16,128]{2,1,0:T(8,128)(2,1)S(1)} %bitcast.39, f32[16]{0:T(128)S(1)} %get-tuple-element.10, f32[16]{0:T(128)S(1)} %get-tuple-element.9), kind=kOutput, calls=%fused_computation.5 | convolution fusion | flops 138413056 | bytes 16777344 | tf_op jit(solution)/shard_map/ja,pak->pjk/dot_general | solution.py:29
  175.5 10.9 %copy.23 = bf16[256,8,16,128]{3,1,2,0:T(8,128)(2,1)} copy(bf16[256,8,16,128]{3,2,1,0:T(8,128)(2,1)} %bitcast.40) | data formatting | bytes 16777216
  186.4 10.6 %fusion = f32[2048,512]{1,0:T(8,128)} fusion(bf16[2048,2048]{1,0:T(8,128)(2,1)} %bitcast.41, f32[2048]{0:T(1024)S(1)} %divide_bitcast_fusion), kind=kOutput, calls=%fused_computation.7 | convolution fusion | flops 4298113024 | bytes 14688256 | tf_op jit(solution)/shard_map/dot_general | solution.py:51
  197.0 0.0 reduce-scatter.2.cloned.1.call-update
  197.0 92.6 %reduce-scatter.2.cloned.1.call-done = f32[128,512]{1,0:T(8,128)} async-done(((f32[2048,512]{1,0:T(8,128)}), f32[128,512]{1,0:T(8,128)}) %reduce-scatter.2.cloned.1.call-update) | async-done | bytes 262160 | tf_op jit(solution)/shard_map/reduce_scatter | solution.py:50
  289.6 1.7 multiply_bitcast_fusion
  (5 shorter events, 0.0 us)
Async XLA Ops:
  21.8 121.9 %all-to-all-start = ((bf16[16,2,8192]{2,1,0:T(2,128)(2,1)}), bf16[16,2,8192]{2,1,0:T(2,128)(2,1)S(1)}, u32[]{:S(2)}, u32[]{:S(2)}) async-start(bf16[16,2,8192]{2,1,0:T(2,128)(2,1)} %reshape.162), calls=%async_computation | async-start | bytes 1048576 | tf_op jit(solution)/shard_map/all_to_all | solution.py:37
  30.2 259.4 %reduce-scatter.2.cloned.1.call-start = ((), (), s32[]{:S(2)}) async-start(), calls=%async_computation.2 | async-start | bytes 4456448 | tf_op jit(solution)/shard_map/reduce_scatter | solution.py:50
Sparse Core Ops, SparseCore 0:
  197.1 92.4 reduce-scatter.1
where the time goes:
time: 299 us; the launch traced here: 298 us
  blocking collectives  108 us (36%)
  waiting for transfers between devices  92.6 us (31%)
  local copies, waits for them, and re-layouts  30.9 us (10%)
  matrix products  22.1 us (7%)
  other arithmetic  20.8 us (7%)
  between operations  14.8 us (5%)
  starting transfers between devices  8.38 us (3%)
    reduce_scatter x1, waiting for transfers between devices, shards(): lax.psum_scatter(lax.dot_general(moved, weighted, (((0,), (0,)), ((), ())...  92.6 us
    all_gather x1, blocking collectives, shards(): lax.all_gather(val_orbitals, ('ka', 'pair'), axis=0, tiled=True)  67.5 us
    unnamed x1, blocking collectives  41 us
    unnamed x8, local copies, waits for them, and re-layouts  15.4 us
    convert_element_type x1, local copies, waits for them, and re-layouts, owner_terms(): pair_real = (picked[:, None, :].astype(jnp.float32) * cond_block[None].as...  13.5 us
    unnamed x1, other arithmetic  11.5 us
    dot_general x1, matrix products, shards(): lax.dot_general(moved, weighted, (((0,), (0,)), ((), ())), preferred_elem...  10.6 us
    all_to_all x1, starting transfers between devices, shards(): lax.all_to_all(cond_orbitals, 'pair', split_axis=2, concat_axis=1, tiled=...  8.34 us
  transfers between devices with their start and end apart: 2, of which 1 were waited for; matrix products, arithmetic and copies ran while one was open for 1% of the time, Pallas kernels for 0%

commit v1 on v0

--- a/solution.py
+++ b/solution.py
@@ -8,6 +8,18 @@
 GB = 128
 WIN = 512
 SLOTS = 16
+
+
+def doubled_up(x, axis, dim):
+    ways, here, turn = (lax.axis_size(axis), lax.axis_index(axis), x.shape[dim])
+    line, have = (x, 1)
+    while have < ways:
+        line = jnp.concatenate(
+            [line, lax.ppermute(line, axis, [(d, (d - have) % ways) for d in range(ways)])],
+            axis=dim,
+        )
+        have = 2 * have
+    return jnp.roll(line, here * turn, axis=dim)
 
 
 def cosine_table(length):
@@ -36,7 +48,7 @@
 def shards(cond_orbitals, cond_energy, val_orbitals, val_energy, val_slots, owner_count):
     cond_block = lax.all_to_all(cond_orbitals, "pair", split_axis=2, concat_axis=1, tiled=True)[0].T
     all_orb, all_energy = (
-        lax.all_gather(val_orbitals, ("ka", "pair"), axis=0, tiled=True),
+        doubled_up(val_orbitals, ("ka", "pair"), 0),
         lax.all_gather(val_energy, ("ka", "pair"), axis=0, tiled=True),
     )
     slots = val_slots[0, 0]

time: 299 us -> 256 us (0.86)
  blocking collectives: 108 us -> 41.5 us
  waiting for transfers between devices: 92.6 us -> 109 us
  starting transfers between devices: 8.38 us -> 11.5 us
    all_gather x1 -> x0, blocking collectives: 67.5 us -> none  [shards(): lax.all_gather(val_orbitals, ('ka', 'pair'), axis=0, tiled=True)]
    ppermute x0 -> x5, waiting for transfers between devices: none -> 11.8 us  [doubled_up(): lax.ppermute(line, axis, [(d, (d - have) % ways) for d in range(ways)])]
    ppermute x0 -> x5, starting transfers between devices: none -> 7.9 us  [doubled_up(): lax.ppermute(line, axis, [(d, (d - have) % ways) for d in range(ways)])]
    reduce_scatter x1, waiting for transfers between devices: 92.6 us -> 97.6 us  [shards(): lax.psum_scatter(lax.dot_general(moved, weighted, (((0,), (0,)), ((), ())...]
    all_to_all x1, starting transfers between devices: 8.34 us -> 3.57 us  [shards(): lax.all_to_all(cond_orbitals, 'pair', split_axis=2, concat_axis=1, tiled=...]
    unnamed x8 -> x7, local copies, waits for them, and re-layouts: 15.4 us -> 15.3 us
  transfers between devices with their start and end apart: 2 -> 7, of which waited for: 1 -> 5; matrix products, arithmetic and copies ran while one was open for 1% -> 9% of each run, Pallas kernels for 0% -> 0%
where the time goes in v1:
time: 256 us; the launch traced here: 255 us
  waiting for transfers between devices  109 us (43%)
  blocking collectives  41.5 us (16%)
  local copies, waits for them, and re-layouts  33.1 us (13%)
  other arithmetic  23 us (9%)
  matrix products  22.1 us (9%)
  between operations  14.9 us (6%)
  starting transfers between devices  11.5 us (4%)
    reduce_scatter x1, waiting for transfers between devices, shards(): lax.psum_scatter(lax.dot_general(moved, weighted, (((0,), (0,)), ((), ())...  97.6 us
    unnamed x1, blocking collectives  41.5 us
    unnamed x7, local copies, waits for them, and re-layouts  15.3 us
    convert_element_type x1, local copies, waits for them, and re-layouts, owner_terms(): pair_real = (picked[:, None, :].astype(jnp.float32) * cond_block[None].as...  13.5 us
    ppermute x5, waiting for transfers between devices, doubled_up(): lax.ppermute(line, axis, [(d, (d - have) % ways) for d in range(ways)])  11.8 us
    unnamed x1, other arithmetic  11.5 us
    dot_general x1, matrix products, shards(): lax.dot_general(moved, weighted, (((0,), (0,)), ((), ())), preferred_elem...  10.6 us
    ppermute x5, starting transfers between devices, doubled_up(): lax.ppermute(line, axis, [(d, (d - have) % ways) for d in range(ways)])  7.9 us
  transfers between devices with their start and end apart: 7, of which 5 were waited for; matrix products, arithmetic and copies ran while one was open for 9% of the time, Pallas kernels for 0%

profile of v1, /device:TPU:0, one launch (start us, length us, event | category | flops | bytes accessed | tf_op | source)
XLA Modules:
  0.0 255.4 jit_solution(10145907756838634918)
XLA Ops:
  6.5 6.4 %collective-permute-start = (bf16[1,2048]{1,0:T(2,128)(2,1)}, bf16[1,2048]{1,0:T(2,128)(2,1)S(1)}, u32[]{:S(2)}, u32[]{:S(2)}) collective-permute-start(bf16[1,2048]{1,0:T(2,128)(2,1)} %param.8), channel_id=1, source_target_pairs={{0,31},{1,0},{2,1},{3,2},{4,3},{5,4},{6,5},{7,6},{8,7},{9,8},{10,9... | collective-permute-start | bytes 12296 | tf_op jit(solution)/shard_map/ppermute | solution.py:18
  12.9 2.3 copy.11
  15.3 0.5 broadcast.174
  15.8 11.5 %reduce = bf16[2048,128]{1,0:T(8,128)(2,1)S(1)} reduce(bf16[2048,1,128]{2,1,0:T(2,128)(2,1)S(1)} %bitcast.39, bf16[]{:T(256)} %broadcast.174), dimensions={1}, to_apply=%bitcast.27.reduce_sub_computation | reduce | bytes 1048578
  27.3 0.9 reshape.160
  28.3 3.6 %all-to-all-start = ((bf16[16,2,8192]{2,1,0:T(2,128)(2,1)}), bf16[16,2,8192]{2,1,0:T(2,128)(2,1)S(1)}, u32[]{:S(2)}, u32[]{:S(2)}) async-start(bf16[16,2,8192]{2,1,0:T(2,128)(2,1)} %reshape.160), calls=%async_computation | async-start | bytes 1048576 | tf_op jit(solution)/shard_map/all_to_all | solution.py:49
  31.9 0.7 fusion.11
  33.4 41.5 %all-reduce = bf16[32]{0:T(256)(128)(2,1)S(1)} all-reduce(bf16[32]{0:T(256)(128)(2,1)S(1)} %dynamic-update-slice), channel_id=1, replica_groups=mesh['ka'=2,'pair'=16] {'ka','pair'}, use_global_device_ids=true, to_apply=%add | all-reduce | flops 32 | bytes 128
  74.8 0.7 gather_fusion.1
  75.5 0.7 select_convert_fusion.1
  76.8 0.7 pad_maximum_fusion.2
  77.5 1.3 collective-permute-start.1
  78.8 2.7 %collective-permute-done.1 = bf16[2,2048]{1,0:T(2,128)(2,1)S(1)} collective-permute-done((bf16[2,2048]{1,0:T(2,128)(2,1)S(1)}, bf16[2,2048]{1,0:T(2,128)(2,1)S(1)}, u32[]{:S(2)}, u32[]{:S(2)}) %collective-permute-start.1) | collective-permute-done | bytes 8224 | tf_op jit(solution)/shard_map/ppermute | solution.py:18
  81.5 0.7 pad_maximum_fusion.1
  82.3 0.7 divide_bitcast_fusion
  83.0 3.1 %collective-permute-done.2 = bf16[4,2048]{1,0:T(4,128)(2,1)S(1)} collective-permute-done((bf16[4,2048]{1,0:T(4,128)(2,1)S(1)}, bf16[4,2048]{1,0:T(4,128)(2,1)S(1)}, u32[]{:S(2)}, u32[]{:S(2)}) %collective-permute-start.2) | collective-permute-done | bytes 16416 | tf_op jit(solution)/shard_map/ppermute | solution.py:18
  86.1 0.7 pad_maximum_fusion
  87.0 4.8 %collective-permute-done.3 = bf16[8,2048]{1,0:T(8,128)(2,1)S(1)} collective-permute-done((bf16[8,2048]{1,0:T(8,128)(2,1)S(1)}, bf16[8,2048]{1,0:T(8,128)(2,1)S(1)}, u32[]{:S(2)}, u32[]{:S(2)}) %collective-permute-start.3) | collective-permute-done | bytes 32800 | tf_op jit(solution)/shard_map/ppermute | solution.py:18
  91.7 0.7 concatenate.25
  92.6 1.2 collective-permute-done.4
  93.8 1.5 concatenate.26
  95.4 0.6 gather_fusion
  96.1 0.5 reshape.161
  96.8 0.3 copy.13
  97.5 5.4 %multiply_convert_fusion = bf16[16,128,2048]{2,1,0:T(8,128)(2,1)} fusion(f32[128,2048]{1,0:T(8,128)S(1)} %copy.14, f32[16,2048]{1,0:T(8,128)S(1)} %select_convert_fusion), kind=kLoop, calls=%fused_computation.3 | loop fusion | flops 8388608 | bytes 9568256 | tf_op jit(solution)/shard_map/convert_element_type | solution.py:36
  102.8 13.5 %convert_element_type.68 = bf16[32768,128]{1,0:T(8,128)(2,1)} reshape(bf16[16,128,2048]{2,1,0:T(8,128)(2,1)} %multiply_convert_fusion) | data formatting | bytes 16777216 | tf_op jit(solution)/shard_map/convert_element_type | solution.py:36
  116.3 5.9 %convolution_convert_fusion = bf16[32768,128]{1,0:T(8,128)(2,1)S(1)} fusion(bf16[32768,128]{1,0:T(8,128)(2,1)} %convert_element_type.68, f32[128]{0:T(128)S(1)} %get-tuple-element.8, f32[128]{0:T(128)S(1)} %get-tuple-element.7), kind=kOutput, calls=%fused_computation.2 | convolution fusion | flops 1078001664 | bytes 16778240 | tf_op jit(solution)/shard_map/dot_general | solution.py:39
  122.2 5.6 %convolution_convert_fusion.1 = bf16[2048,128,16]{1,2,0:T(8,128)(2,1)} fusion(bf16[2048,16,128]{2,1,0:T(8,128)(2,1)S(1)} %bitcast.35, f32[16]{0:T(128)S(1)} %get-tuple-element.10, f32[16]{0:T(128)S(1)} %get-tuple-element.9), kind=kOutput, calls=%fused_computation.5 | convolution fusion | flops 138413056 | bytes 16777344 | tf_op jit(solution)/shard_map/ja,pak->pjk/dot_general | solution.py:41
  127.8 10.9 %copy.17 = bf16[256,8,16,128]{3,1,2,0:T(8,128)(2,1)} copy(bf16[256,8,16,128]{3,2,1,0:T(8,128)(2,1)} %bitcast.36) | data formatting | bytes 16777216
  138.7 10.6 %fusion = f32[2048,512]{1,0:T(8,128)} fusion(bf16[2048,2048]{1,0:T(8,128)(2,1)} %bitcast.37, f32[2048]{0:T(1024)S(1)} %divide_bitcast_fusion), kind=kOutput, calls=%fused_computation.7 | convolution fusion | flops 4298113024 | bytes 14688256 | tf_op jit(solution)/shard_map/dot_general | solution.py:63
  149.3 97.6 %reduce-scatter.2.cloned.1.call-done = f32[128,512]{1,0:T(8,128)} async-done(((f32[2048,512]{1,0:T(8,128)}), f32[128,512]{1,0:T(8,128)}) %reduce-scatter.2.cloned.1.call-update) | async-done | bytes 262160 | tf_op jit(solution)/shard_map/reduce_scatter | solution.py:62
  246.9 1.7 multiply_bitcast_fusion
  (18 shorter events, 1.0 us)
Async XLA Ops:
  6.5 70.3 %collective-permute-start = (bf16[1,2048]{1,0:T(2,128)(2,1)}, bf16[1,2048]{1,0:T(2,128)(2,1)S(1)}, u32[]{:S(2)}, u32[]{:S(2)}) collective-permute-start(bf16[1,2048]{1,0:T(2,128)(2,1)} %param.8), channel_id=1, source_target_pairs={{0,31},{1,0},{2,1},{3,2},{4,3},{5,4},{6,5},{7,6},{8,7},{9,8},{10,9... | collective-permute-start | bytes 12296 | tf_op jit(solution)/shard_map/ppermute | solution.py:18
  28.3 67.8 %all-to-all-start = ((bf16[16,2,8192]{2,1,0:T(2,128)(2,1)}), bf16[16,2,8192]{2,1,0:T(2,128)(2,1)S(1)}, u32[]{:S(2)}, u32[]{:S(2)}) async-start(bf16[16,2,8192]{2,1,0:T(2,128)(2,1)} %reshape.160), calls=%async_computation | async-start | bytes 1048576 | tf_op jit(solution)/shard_map/all_to_all | solution.py:49
  31.8 215.0 %reduce-scatter.2.cloned.1.call-start = ((), (), s32[]{:S(2)}) async-start(), calls=%async_computation.2 | async-start | bytes 4456448 | tf_op jit(solution)/shard_map/reduce_scatter | solution.py:62
  77.5 4.0 %collective-permute-start.1 = (bf16[2,2048]{1,0:T(2,128)(2,1)S(1)}, bf16[2,2048]{1,0:T(2,128)(2,1)S(1)}, u32[]{:S(2)}, u32[]{:S(2)}) collective-permute-start(bf16[2,2048]{1,0:T(2,128)(2,1)S(1)} %pad_maximum_fusion.2), channel_id=1, source_target_pairs={{0,30},{1,31},{2,0},{3,1},{4,2},{5,3},{6,4},{7,5},{8,6},{9,7},{10,... | collective-permute-start | bytes 24584 | tf_op jit(solution)/shard_map/ppermute | solution.py:18
  82.2 3.9 %collective-permute-start.2 = (bf16[4,2048]{1,0:T(4,128)(2,1)S(1)}, bf16[4,2048]{1,0:T(4,128)(2,1)S(1)}, u32[]{:S(2)}, u32[]{:S(2)}) collective-permute-start(bf16[4,2048]{1,0:T(4,128)(2,1)S(1)} %pad_maximum_fusion.1), channel_id=1, source_target_pairs={{0,28},{1,29},{2,30},{3,31},{4,0},{5,1},{6,2},{7,3},{8,4},{9,5},{1... | collective-permute-start | bytes 49160 | tf_op jit(solution)/shard_map/ppermute | solution.py:18
  86.9 4.9 %collective-permute-start.3 = (bf16[8,2048]{1,0:T(8,128)(2,1)S(1)}, bf16[8,2048]{1,0:T(8,128)(2,1)S(1)}, u32[]{:S(2)}, u32[]{:S(2)}) collective-permute-start(bf16[8,2048]{1,0:T(8,128)(2,1)S(1)} %pad_maximum_fusion), channel_id=1, source_target_pairs={{0,24},{1,25},{2,26},{3,27},{4,28},{5,29},{6,30},{7,31},{8,0},{9,1... | collective-permute-start | bytes 98312 | tf_op jit(solution)/shard_map/ppermute | solution.py:18
  92.5 1.3 collective-permute-start.4
Sparse Core Ops, SparseCore 0:
  149.4 97.3 reduce-scatter.1
